TPU v7x, 32 devices: a whole 2x2x4 slice. The times are simulated.
32 devices in a mesh: cuts: 2 (over x), mode: 8 (over z, y), branch: 2 (over core).
Axes of the slice: x: 2, y: 2, z: 4, core: 2. Of those that a mesh axis runs over, the one named last changes fastest.
Arguments:
- leaves: bfloat16 [8, 2, 32, 512, 512], P('branch', None, ('cuts', 'mode')), parts along dimension 2, may hold values from -0.1875 to 0.1875
- join_order: int32 [7], replicated, may hold values from 0 to 1
- slice_values: int32 [32], P(('cuts', 'mode')), parts along dimension 0, may hold values from 0 to 1
- boundary: bfloat16 [2, 2, 512, 512], replicated, may hold values from -4 to 4
Outputs:
- amplitudes: float32 [2, 32, 512, 512], P(None, ('cuts', 'mode'), 'branch'), parts along dimension 1
There are 2 independent parts, one for each index of `cuts`. A program takes and returns all parts, laid end to end along the dimension named above; an argument that names none is the same for every part. Nothing has to cross between parts.
Inputs may be any that keep to these rules, and one draw needn't show every extreme that they name: `join_order`: 1 puts the second operand of the join on the left.
All inputs are finite; a program needn't handle non-finite values.
Results may differ from a plain program's by a relative error of at most 0.0076.
Values may be sent and summed in bfloat16 or wider, within the bound.
A program may use at most 64 MiB of HBM per device.

v0:
```python
import jax
import jax.numpy as jnp
from jax import lax
from jax.sharding import PartitionSpec as P


def from_partner(value, axis, bit):
    mask = 2**bit
    pairs = [(source, source ^ mask) for source in range(lax.axis_size(axis))]
    return lax.ppermute(value, axis, pairs)


def complex_sums(left_op, right_op):
    spec = "bij,bjk->bik"
    real_part = jnp.einsum(
        spec, left_op[0], right_op[0], preferred_element_type=jnp.float32
    ) - jnp.einsum(spec, left_op[1], right_op[1], preferred_element_type=jnp.float32)
    imag_part = jnp.einsum(
        spec, left_op[0], right_op[1], preferred_element_type=jnp.float32
    ) + jnp.einsum(spec, left_op[1], right_op[0], preferred_element_type=jnp.float32)
    return jnp.stack([real_part, imag_part])


def complex_product(left_op, right_op):
    return complex_sums(left_op, right_op).astype(jnp.bfloat16)


def join_pair(left_op, right_op, swapped):
    return lax.cond(
        swapped == 1,
        lambda: complex_product(right_op, left_op),
        lambda: complex_product(left_op, right_op),
    )


def split_rows(tensor, blocks):
    shape = tensor.shape
    return tensor.reshape(shape[0], shape[1], blocks, shape[2] // blocks, shape[3])


def merge_rows(tensor):
    shape = tensor.shape
    width = shape[4]
    total_rows = shape[1] * shape[2] * shape[3]
    return tensor.reshape(shape[0], total_rows // width, width, width)


def per_device(leaves, join_order, slice_values, boundary):
    blocks = lax.axis_size("mode")
    branch_index = lax.axis_index("branch")
    base_index = 2 * branch_index
    first_pair = join_pair(leaves[0], leaves[1], join_order[base_index])
    second_pair = join_pair(leaves[2], leaves[3], join_order[base_index + 1])
    first_pair, second_pair = (
        lax.all_to_all(
            split_rows(first_pair, blocks), "mode", split_axis=2, concat_axis=1, tiled=True
        ),
        lax.all_to_all(
            split_rows(second_pair, blocks), "mode", split_axis=2, concat_axis=1, tiled=True
        ),
    )
    first_pair = merge_rows(first_pair)
    second_pair = merge_rows(second_pair)
    middle = join_pair(first_pair, second_pair, join_order[4 + branch_index])
    middle = merge_rows(
        lax.all_to_all(split_rows(middle, blocks), "mode", split_axis=2, concat_axis=1, tiled=True)
    )
    width = middle.shape[3]
    half_rows = width // 2
    chosen = jnp.where(
        slice_values[None, :, None, None] == 1, boundary[1][:, None], boundary[0][:, None]
    )
    top_order = join_order[-1]
    partner = from_partner(middle, "branch", 0)
    is_first = branch_index == 0
    upper = jnp.where(is_first, middle, partner)
    lower = jnp.where(is_first, partner, middle)
    leading = jnp.where(top_order == 1, lower, upper)
    trailing = jnp.where(top_order == 1, upper, lower)
    leading = lax.dynamic_slice_in_dim(leading, branch_index * half_rows, half_rows, 2)
    top_half = complex_product(leading, trailing)
    amplitudes = complex_sums(top_half, chosen)
    return amplitudes


def solution(mesh):
    in_specs = (P("branch", None, ("cuts", "mode"), None, None), P(), P(("cuts", "mode")), P())
    out_specs = P(None, ("cuts", "mode"), "branch", None)
    return jax.shard_map(
        per_device, mesh=mesh, in_specs=in_specs, out_specs=out_specs, check_vma=False
    )
```

profile of v0, /device:TPU:0, one launch (start us, length us, event | category | flops | bytes accessed | tf_op | source)
XLA Modules:
  0.0 195.7 jit_solution(156778789101351986)
XLA Ops:
  0.0 5.7 %slice_bitcast_fusion = (bf16[2,2,512,512]{3,2,1,0:T(8,128)(2,1)}, bf16[2,2,512,512]{3,2,1,0:T(8,128)(2,1)S(1)}, bf16[2,2,512,512]{3,2,1,0:T(8,128)(2,1)}, bf16[2,2,512,512]{3,2,1,0:T(8,128)(2,1)}) fusion(bf16[4,2,2,512,512]{4,3,2,1,0:T(8,128)(2,1)} %param.10), kind=kLoop, calls=%fused_computation.127 | loop fusion | bytes 16777216 | tf_op jit(solution)/shard_map/squeeze | solution.py:53
  5.7 0.7 fusion.116
  7.0 6.6 %conditional.7 = (bf16[2,2,512,512]{3,2,1,0:T(8,128)(2,1)}) conditional(s32[]{:T(128)} %bitcast.45, (bf16[2,2,512,512]{3,2,1,0:T(8,128)(2,1)}, bf16[2,2,512,512]{3,2,1,0:T(8,128)(2,1)}) %tuple.34, (bf16[2,2,512,512]{3,2,1,0:T(8,128)(2,1)}, bf16[2,2,512,512]{3,2,1,0:T(8,128)(2,1)}) %tuple.35), branch_computations={%region_2.0_spmd, %region_3.0_spmd} | conditional | flops 2150629376 | bytes 39845952
  7.0 0.0 copy-start.2
  7.1 2.4 %fusion.36 = f32[2,512,512]{2,1,0:T(8,128)S(1)} fusion(bf16[2,2,512,512]{3,2,1,0:T(8,128)(2,1)} %get-tuple-element.49, bf16[2,2,512,512]{3,2,1,0:T(8,128)(2,1)} %get-tuple-element.48), kind=kOutput, calls=%fused_computation.45 | convolution fusion | flops 536870912 | bytes 4194304 | tf_op jit(solution)/shard_map/cond/branch_0_fun/bij,bjk->bik/dot_general | solution.py:18
  9.5 0.4 copy-done.4
  9.9 0.7 add_bitcast_fusion.2
  10.6 0.7 fusion.42
  11.3 0.7 subtract_bitcast_fusion.2
  12.1 1.6 pad_maximum_fusion.2
  13.6 3.2 %copy.11 = bf16[2,2,8,64,512]{4,3,1,0,2:T(8,128)(2,1)} copy(bf16[2,2,8,64,512]{4,3,2,1,0:T(8,128)(2,1)} %bitcast.213) | data formatting | bytes 4194304 | tf_op jit(solution)/shard_map/reshape | solution.py:38
  16.8 7.3 %all-to-all-start.1 = ((bf16[2,2,8,64,512]{4,3,1,0,2:T(8,128)(2,1)}), bf16[2,2,8,64,512]{4,3,1,0,2:T(8,128)(2,1)}, u32[]{:S(2)}, u32[]{:S(2)}) async-start(bf16[2,2,8,64,512]{4,3,1,0,2:T(8,128)(2,1)} %copy.11), calls=%async_computation.1 | async-start | bytes 4194304 | tf_op jit(solution)/shard_map/all_to_all | solution.py:58
  24.7 4.5 %conditional.6 = (bf16[2,2,512,512]{3,2,1,0:T(8,128)(2,1)S(1)}) conditional(s32[]{:T(128)} %bitcast.38, (bf16[2,2,512,512]{3,2,1,0:T(8,128)(2,1)}, bf16[2,2,512,512]{3,2,1,0:T(8,128)(2,1)S(1)}) %tuple.32, (bf16[2,2,512,512]{3,2,1,0:T(8,128)(2,1)S(1)}, bf16[2,2,512,512]{3,2,1,0:T(8,128)(2,1)}) %tuple.33), branch_computations={%region_0.0_spmd, %region_1.0_spmd} | conditional | flops 2150629376 | bytes 31457316
  24.8 2.1 %fusion.18 = f32[2,512,512]{2,1,0:T(8,128)S(1)} fusion(bf16[2,2,512,512]{3,2,1,0:T(8,128)(2,1)} %get-tuple-element.47, bf16[2,2,512,512]{3,2,1,0:T(8,128)(2,1)S(1)} %get-tuple-element.46), kind=kOutput, calls=%fused_computation.24 | convolution fusion | flops 536870912 | bytes 4194304 | tf_op jit(solution)/shard_map/cond/branch_1_fun/bij,bjk->bik/dot_general | solution.py:18
  26.9 0.7 add_bitcast_fusion.1
  27.6 0.7 fusion.24
  28.3 0.7 subtract_bitcast_fusion.1
  29.0 0.2 pad_maximum_fusion.1
  29.2 1.5 copy.9
  30.7 41.7 %all-to-all-done.1 = bf16[2,2,8,64,512]{4,3,1,0,2:T(8,128)(2,1)} async-done(((bf16[2,2,8,64,512]{4,3,1,0,2:T(8,128)(2,1)}), bf16[2,2,8,64,512]{4,3,1,0,2:T(8,128)(2,1)}, u32[]{:S(2)}, u32[]{:S(2)}) %all-to-all-start.1) | async-done | bytes 2097184 | tf_op jit(solution)/shard_map/all_to_all | solution.py:58
  72.4 4.4 %all-to-all-start = ((bf16[2,2,8,64,512]{4,3,1,0,2:T(8,128)(2,1)}), bf16[2,2,8,64,512]{4,3,1,0,2:T(8,128)(2,1)}, u32[]{:S(2)}, u32[]{:S(2)}) async-start(bf16[2,2,8,64,512]{4,3,1,0,2:T(8,128)(2,1)} %copy.9), calls=%async_computation | async-start | bytes 4194304 | tf_op jit(solution)/shard_map/all_to_all | solution.py:55
  77.5 1.8 copy.12
  79.3 45.3 %all-to-all-done = bf16[2,2,8,64,512]{4,3,1,0,2:T(8,128)(2,1)} async-done(((bf16[2,2,8,64,512]{4,3,1,0,2:T(8,128)(2,1)}), bf16[2,2,8,64,512]{4,3,1,0,2:T(8,128)(2,1)}, u32[]{:S(2)}, u32[]{:S(2)}) %all-to-all-start) | async-done | bytes 2097184 | tf_op jit(solution)/shard_map/all_to_all | solution.py:55
  124.6 1.8 copy.10
  126.4 3.3 %conditional.8 = (bf16[2,2,512,512]{3,2,1,0:T(8,128)(2,1)S(1)}) conditional(s32[]{:T(128)} %bitcast.37, (bf16[2,2,512,512]{3,2,1,0:T(8,128)(2,1)S(1)}, bf16[2,2,512,512]{3,2,1,0:T(8,128)(2,1)S(1)}) %tuple.55, (bf16[2,2,512,512]{3,2,1,0:T(8,128)(2,1)S(1)}, bf16[2,2,512,512]{3,2,1,0:T(8,128)(2,1)S(1)}) %tuple.56), branch_computations={%region_4.0_spmd, %region_5.0_spmd} | conditional | flops 2150629376 | bytes 23068680
  126.4 0.7 fusion.72
  127.2 0.7 add_bitcast_fusion.4
  127.9 0.7 fusion.78
  128.6 0.7 subtract_bitcast_fusion.4
  129.3 0.2 pad_maximum_fusion.4
  129.7 0.2 copy.13
  129.9 51.8 %all_to_all.45 = bf16[2,2,8,64,512]{4,3,1,0,2:T(8,128)(2,1)S(1)} all-to-all(bf16[2,2,8,64,512]{4,3,1,0,2:T(8,128)(2,1)S(1)} %copy.13), channel_id=1, replica_groups=mesh['cuts'=2,'mode'=8,'branch'=2] {'mode'}, dimensions={2} | all-to-all | bytes 4194304 | tf_op jit(solution)/shard_map/all_to_all | solution.py:66
  181.7 1.5 copy.14
  183.3 0.0 collective-permute-start
  183.9 1.7 slice_bitcast_fusion.9
  185.6 0.3 broadcast_select_fusion
  185.9 1.9 collective-permute-done
  187.8 2.6 %broadcast_select_fusion.3 = (bf16[2,2,512,512]{3,2,1,0:T(8,128)(2,1)S(1)}, bf16[2,2,512,512]{3,2,1,0:T(8,128)(2,1)S(1)}, bf16[2,2,512,512]{3,2,1,0:T(8,128)(2,1)S(1)}) fusion(pred[]{:T(512)} %bitcast.36, bf16[2,2,512,512]{3,2,1,0:T(8,128)(2,1)} %collective-permute-done, bf16[2,2,512,512]{3,2,1,0:T(8,128)(2,1)} %bitcast.59, pred[]{:T(512)S(6)} %eq.28), kind=kLoop, calls=%fused_computation.134 | loop fusion | flops 3145728 | bytes 10485762 | tf_op jit(solution)/shard_map/jit(_where)/select_n | solution.py:79
  190.4 0.3 dynamic-slice_select_fusion
  190.7 0.4 fusion.113
  191.1 0.4 fusion.112
  191.6 0.4 fusion.110
  192.0 0.4 fusion.114
  192.5 0.4 fusion.115
  192.9 0.4 fusion.111
  193.4 0.4 fusion.109
  193.8 0.4 fusion.108
  194.2 1.5 pad_maximum_fusion.6
  (9 shorter events, 0.0 us)
Async XLA Ops:
  0.0 5.7 %copy-start.6 = (s32[7]{0:T(128)S(1)}, s32[7]{0:T(128)}, u32[]{:S(2)}) copy-start(s32[7]{0:T(128)} %param.11) | copy-start | bytes 88
  7.0 2.4 %copy-start.2 = (bf16[2,2,512,512]{3,2,1,0:T(8,128)(2,1)S(1)}, bf16[2,2,512,512]{3,2,1,0:T(8,128)(2,1)}, u32[]{:S(2)}) copy-start(bf16[2,2,512,512]{3,2,1,0:T(8,128)(2,1)} %get-tuple-element.49) | copy-start | bytes 6291460 | tf_op jit(solution)/shard_map/conditional.1
  7.1 2.8 %copy-start.4 = (bf16[2,2,512,512]{3,2,1,0:T(8,128)(2,1)S(1)}, bf16[2,2,512,512]{3,2,1,0:T(8,128)(2,1)}, u32[]{:S(2)}) copy-start(bf16[2,2,512,512]{3,2,1,0:T(8,128)(2,1)} %get-tuple-element.48) | copy-start | bytes 6291460 | tf_op jit(solution)/shard_map/conditional.1
  16.8 55.7 %all-to-all-start.1 = ((bf16[2,2,8,64,512]{4,3,1,0,2:T(8,128)(2,1)}), bf16[2,2,8,64,512]{4,3,1,0,2:T(8,128)(2,1)}, u32[]{:S(2)}, u32[]{:S(2)}) async-start(bf16[2,2,8,64,512]{4,3,1,0,2:T(8,128)(2,1)} %copy.11), calls=%async_computation.1 | async-start | bytes 4194304 | tf_op jit(solution)/shard_map/all_to_all | solution.py:58
  24.8 2.1 %copy-start.1 = (bf16[2,2,512,512]{3,2,1,0:T(8,128)(2,1)S(1)}, bf16[2,2,512,512]{3,2,1,0:T(8,128)(2,1)}, u32[]{:S(2)}) copy-start(bf16[2,2,512,512]{3,2,1,0:T(8,128)(2,1)} %get-tuple-element.47) | copy-start | bytes 6291460 | tf_op jit(solution)/shard_map/conditional
  72.4 52.2 %all-to-all-start = ((bf16[2,2,8,64,512]{4,3,1,0,2:T(8,128)(2,1)}), bf16[2,2,8,64,512]{4,3,1,0,2:T(8,128)(2,1)}, u32[]{:S(2)}, u32[]{:S(2)}) async-start(bf16[2,2,8,64,512]{4,3,1,0,2:T(8,128)(2,1)} %copy.9), calls=%async_computation | async-start | bytes 4194304 | tf_op jit(solution)/shard_map/all_to_all | solution.py:55
  181.7 2.2 %copy-start.7 = (s32[2]{0:T(128)S(1)}, s32[2]{0:T(128)}, u32[]{:S(2)}) copy-start(s32[2]{0:T(128)} %param.12) | copy-start | bytes 28
  183.3 4.5 %collective-permute-start = (bf16[2,2,512,512]{3,2,1,0:T(8,128)(2,1)}, bf16[2,2,512,512]{3,2,1,0:T(8,128)(2,1)}, u32[]{:S(2)}, u32[]{:S(2)}) collective-permute-start(bf16[2,2,512,512]{3,2,1,0:T(8,128)(2,1)} %bitcast.59), channel_id=1, source_target_pairs={{0,1},{1,0},{2,3},{3,2},{4,5},{5,4},{6,7},{7,6},{8,9},{9,8},{10,11... | collective-permute-start | bytes 6291464 | tf_op jit(solution)/shard_map/ppermute | solution.py:10
where the time goes:
time: 196 us
  waiting for transfers between devices  88.9 us (45%)
  blocking collectives  51.8 us (26%)
  local copies, waits for them, and re-layouts  18.6 us (9%)
  matrix products  15.1 us (8%)
  starting transfers between devices  11.7 us (6%)
  other arithmetic  6.63 us (3%)
  between operations  2.74 us (1%)
    all_to_all x1, blocking collectives, per_device(): lax.all_to_all(split_rows(middle, blocks), 'mode', split_axis=2, concat_a...  51.8 us
    all_to_all x1, waiting for transfers between devices, per_device(): lax.all_to_all(split_rows(first_pair, blocks), 'mode', split_axis=2, conc...  45.3 us
    all_to_all x1, waiting for transfers between devices, per_device(): lax.all_to_all(split_rows(second_pair, blocks), 'mode', split_axis=2, con...  41.7 us
    all_to_all x1, starting transfers between devices, per_device(): lax.all_to_all(split_rows(second_pair, blocks), 'mode', split_axis=2, con...  7.31 us
    dot_general x5, matrix products, complex_sums(): jnp.einsum(spec, left_op[0], right_op[1], preferred_element_type=jnp.floa...  6.06 us
    squeeze x1, local copies, waits for them, and re-layouts, per_device(): second_pair = join_pair(leaves[2], leaves[3], join_order[base_index + 1])  5.73 us
    reshape x3, local copies, waits for them, and re-layouts, split_rows(): tensor.reshape(shape[0], shape[1], blocks, shape[2] // blocks, shape[3])  4.91 us
    all_to_all x1, starting transfers between devices, per_device(): lax.all_to_all(split_rows(first_pair, blocks), 'mode', split_axis=2, conc...  4.35 us
  transfers between devices with their start and end apart: 3, of which 3 were waited for; matrix products, arithmetic and copies ran while one was open for 5% of the time, Pallas kernels for 0%

commit v1 on v0

--- a/solution.py
+++ b/solution.py
@@ -2,6 +2,18 @@
 import jax.numpy as jnp
 from jax import lax
 from jax.sharding import PartitionSpec as P
+
+
+def exchange_directly(x, axis, split, join):
+    ways, here = (lax.axis_size(axis), lax.axis_index(axis))
+    width = x.shape[split] // ways
+    turned = jnp.roll(x, -here * width, axis=split)
+    got = [lax.slice_in_dim(turned, 0, width, axis=split)]
+    for far in range(1, ways):
+        sent = lax.slice_in_dim(turned, far * width, (far + 1) * width, axis=split)
+        got.append(lax.ppermute(sent, axis, [(d, (d + far) % ways) for d in range(ways)]))
+    line = jnp.concatenate(got[::-1], axis=join)
+    return jnp.roll(line, (here + 1) * got[0].shape[join], axis=join)
 
 
 def from_partner(value, axis, bit):
@@ -55,9 +67,7 @@
         lax.all_to_all(
             split_rows(first_pair, blocks), "mode", split_axis=2, concat_axis=1, tiled=True
         ),
-        lax.all_to_all(
-            split_rows(second_pair, blocks), "mode", split_axis=2, concat_axis=1, tiled=True
-        ),
+        exchange_directly(split_rows(second_pair, blocks), "mode", 2, 1),
     )
     first_pair = merge_rows(first_pair)
     second_pair = merge_rows(second_pair)

time: 196 us -> 187 us (0.954)
  waiting for transfers between devices: 88.9 us -> 44.5 us
  starting transfers between devices: 11.7 us -> 47.9 us
    all_to_all x1, waiting for transfers between devices: 45.3 us -> 0.01 us  [per_device(): lax.all_to_all(split_rows(first_pair, blocks), 'mode', split_axis=2, conc...]
    ppermute x0 -> x7, waiting for transfers between devices: none -> 42.7 us  [exchange_directly(): lax.ppermute(sent, axis, [(d, (d + far) % ways) for d in range(ways)])]
    all_to_all x1 -> x0, waiting for transfers between devices: 41.7 us -> none  [per_device(): lax.all_to_all(split_rows(second_pair, blocks), 'mode', split_axis=2, con...]
    ppermute x0 -> x7, starting transfers between devices: none -> 40.5 us  [exchange_directly(): lax.ppermute(sent, axis, [(d, (d + far) % ways) for d in range(ways)])]
    all_to_all x1 -> x0, starting transfers between devices: 7.31 us -> none  [per_device(): lax.all_to_all(split_rows(second_pair, blocks), 'mode', split_axis=2, con...]
    all_to_all x1, starting transfers between devices: 4.35 us -> 7.31 us  [per_device(): lax.all_to_all(split_rows(first_pair, blocks), 'mode', split_axis=2, conc...]
    unnamed x4 -> x22, local copies, waits for them, and re-layouts: 0.01 us -> 2.88 us
    concatenate x0 -> x1, other arithmetic: none -> 2.34 us  [exchange_directly(): turned = jnp.roll(x, -here * width, axis=split)]
  transfers between devices with their start and end apart: 3 -> 9, of which waited for: 3 -> 5; matrix products, arithmetic and copies ran while one was open for 5% -> 6% of each run, Pallas kernels for 0% -> 0%
where the time goes in v1:
time: 187 us; the launch traced here: 186 us
  blocking collectives  50.3 us (27%)
  starting transfers between devices  47.9 us (26%)
  waiting for transfers between devices  44.5 us (24%)
  local copies, waits for them, and re-layouts  17 us (9%)
  matrix products  15.1 us (8%)
  other arithmetic  8.33 us (4%)
  between operations  2.79 us (1%)
    all_to_all x1, blocking collectives, per_device(): lax.all_to_all(split_rows(middle, blocks), 'mode', split_axis=2, concat_a...  50.3 us
    ppermute x7, waiting for transfers between devices, exchange_directly(): lax.ppermute(sent, axis, [(d, (d + far) % ways) for d in range(ways)])  42.7 us
    ppermute x7, starting transfers between devices, exchange_directly(): lax.ppermute(sent, axis, [(d, (d + far) % ways) for d in range(ways)])  40.5 us
    all_to_all x1, starting transfers between devices, per_device(): lax.all_to_all(split_rows(first_pair, blocks), 'mode', split_axis=2, conc...  7.31 us
    dot_general x5, matrix products, complex_sums(): jnp.einsum(spec, left_op[0], right_op[1], preferred_element_type=jnp.floa...  6.06 us
    squeeze x1, local copies, waits for them, and re-layouts, per_device(): second_pair = join_pair(leaves[2], leaves[3], join_order[base_index + 1])  5.7 us
  transfers between devices with their start and end apart: 9, of which 5 were waited for; matrix products, arithmetic and copies ran while one was open for 6% of the time, Pallas kernels for 0%

profile of v1, /device:TPU:0, one launch (start us, length us, event | category | flops | bytes accessed | tf_op | source)
XLA Modules:
  0.0 186.2 jit_solution(7001037594515468208)
XLA Ops:
  0.0 5.7 %slice_bitcast_fusion = (bf16[2,2,512,512]{3,2,1,0:T(8,128)(2,1)S(1)}, bf16[2,2,512,512]{3,2,1,0:T(8,128)(2,1)}, bf16[2,2,512,512]{3,2,1,0:T(8,128)(2,1)}, bf16[2,2,512,512]{3,2,1,0:T(8,128)(2,1)}) fusion(bf16[4,2,2,512,512]{4,3,2,1,0:T(8,128)(2,1)} %param.10), kind=kLoop, calls=%fused_computation.130 | loop fusion | bytes 16777216 | tf_op jit(solution)/shard_map/squeeze | solution.py:65
  5.7 0.7 fusion.119
  7.0 6.6 %conditional.6 = (bf16[2,2,512,512]{3,2,1,0:T(8,128)(2,1)}) conditional(s32[]{:T(128)} %bitcast.38, (bf16[2,2,512,512]{3,2,1,0:T(8,128)(2,1)}, bf16[2,2,512,512]{3,2,1,0:T(8,128)(2,1)}) %tuple.32, (bf16[2,2,512,512]{3,2,1,0:T(8,128)(2,1)}, bf16[2,2,512,512]{3,2,1,0:T(8,128)(2,1)}) %tuple.33), branch_computations={%region_0.0_spmd, %region_1.0_spmd} | conditional | flops 2150629376 | bytes 39845952
  7.0 2.4 %fusion.18 = f32[2,512,512]{2,1,0:T(8,128)S(1)} fusion(bf16[2,2,512,512]{3,2,1,0:T(8,128)(2,1)} %get-tuple-element.47, bf16[2,2,512,512]{3,2,1,0:T(8,128)(2,1)} %get-tuple-element.46), kind=kOutput, calls=%fused_computation.24 | convolution fusion | flops 536870912 | bytes 4194304 | tf_op jit(solution)/shard_map/cond/branch_1_fun/bij,bjk->bik/dot_general | solution.py:30
  9.5 0.4 copy-done.5
  9.9 0.7 add_bitcast_fusion.1
  10.6 0.7 fusion.24
  11.3 0.7 subtract_bitcast_fusion.1
  12.0 1.6 pad_maximum_fusion.1
  13.6 3.1 %copy.12 = bf16[2,2,8,64,512]{4,3,1,0,2:T(8,128)(2,1)} copy(bf16[2,2,8,64,512]{4,3,2,1,0:T(8,128)(2,1)} %bitcast.229) | data formatting | bytes 4194304 | tf_op jit(solution)/shard_map/reshape | solution.py:50
  16.7 7.3 %all-to-all-start = ((bf16[2,2,8,64,512]{4,3,1,0,2:T(8,128)(2,1)}), bf16[2,2,8,64,512]{4,3,1,0,2:T(8,128)(2,1)}, u32[]{:S(2)}, u32[]{:S(2)}) async-start(bf16[2,2,8,64,512]{4,3,1,0,2:T(8,128)(2,1)} %copy.12), calls=%async_computation | async-start | bytes 4194304 | tf_op jit(solution)/shard_map/all_to_all | solution.py:67
  24.7 4.5 %conditional.7 = (bf16[2,2,512,512]{3,2,1,0:T(8,128)(2,1)S(1)}) conditional(s32[]{:T(128)} %bitcast.45, (bf16[2,2,512,512]{3,2,1,0:T(8,128)(2,1)}, bf16[2,2,512,512]{3,2,1,0:T(8,128)(2,1)S(1)}) %tuple.34, (bf16[2,2,512,512]{3,2,1,0:T(8,128)(2,1)S(1)}, bf16[2,2,512,512]{3,2,1,0:T(8,128)(2,1)}) %tuple.35), branch_computations={%region_2.0_spmd, %region_3.0_spmd} | conditional | flops 2150629376 | bytes 31457316
  24.7 2.1 %fusion.36 = f32[2,512,512]{2,1,0:T(8,128)S(1)} fusion(bf16[2,2,512,512]{3,2,1,0:T(8,128)(2,1)S(1)} %get-tuple-element.49, bf16[2,2,512,512]{3,2,1,0:T(8,128)(2,1)} %get-tuple-element.48), kind=kOutput, calls=%fused_computation.45 | convolution fusion | flops 536870912 | bytes 4194304 | tf_op jit(solution)/shard_map/cond/branch_0_fun/bij,bjk->bik/dot_general | solution.py:30
  26.8 0.7 add_bitcast_fusion.2
  27.5 0.7 fusion.42
  28.2 0.7 subtract_bitcast_fusion.2
  29.1 1.3 copy-done.6
  30.4 2.3 %fusion.108 = bf16[2,2,8,64,512]{4,3,2,1,0:T(8,128)(2,1)S(1)} fusion(s32[]{:T(128)S(6)} %select_n.67, bf16[2,2,8,64,512]{4,3,2,1,0:T(8,128)(2,1)} %bitcast.230), kind=kLoop, calls=%fused_computation.128 | loop fusion | flops 1048576 | bytes 4194308 | tf_op jit(solution)/shard_map/jit(_roll_dynamic)/concatenate | solution.py:10
  32.8 1.3 slice_bitcast_fusion.25
  34.1 4.7 %collective-permute-start = (bf16[2,2,1,64,512]{4,3,1,0,2:T(8,128)(2,1)}, bf16[2,2,1,64,512]{4,3,1,0,2:T(8,128)(2,1)S(1)}, u32[]{:S(2)}, u32[]{:S(2)}) collective-permute-start(bf16[2,2,1,64,512]{4,3,1,0,2:T(8,128)(2,1)} %get-tuple-element.71), channel_id=1, source_target_pairs={{0,14},{2,0},{4,2},{6,4},{8,6},{10,8},{12,10},{14,12},{1,15},{3,1}... | collective-permute-start | bytes 786440 | tf_op jit(solution)/shard_map/ppermute | solution.py:14
  38.8 0.5 collective-permute-start.1
  39.3 2.9 %collective-permute-start.3 = (bf16[2,2,1,64,512]{4,3,1,0,2:T(8,128)(2,1)}, bf16[2,2,1,64,512]{4,3,1,0,2:T(8,128)(2,1)S(1)}, u32[]{:S(2)}, u32[]{:S(2)}) collective-permute-start(bf16[2,2,1,64,512]{4,3,1,0,2:T(8,128)(2,1)} %get-tuple-element.68), channel_id=1, source_target_pairs={{0,8},{2,10},{4,12},{6,14},{8,0},{10,2},{12,4},{14,6},{1,9},{3,11}... | collective-permute-start | bytes 786440 | tf_op jit(solution)/shard_map/ppermute | solution.py:14
  42.9 23.0 %collective-permute-done = bf16[2,2,1,64,512]{4,3,1,0,2:T(8,128)(2,1)S(1)} collective-permute-done((bf16[2,2,1,64,512]{4,3,1,0,2:T(8,128)(2,1)}, bf16[2,2,1,64,512]{4,3,1,0,2:T(8,128)(2,1)S(1)}, u32[]{:S(2)}, u32[]{:S(2)}) %collective-permute-start) | collective-permute-done | bytes 262176 | tf_op jit(solution)/shard_map/ppermute | solution.py:14
  65.9 5.6 %collective-permute-done.1 = bf16[2,2,1,64,512]{4,3,1,0,2:T(8,128)(2,1)S(1)} collective-permute-done((bf16[2,2,1,64,512]{4,3,1,0,2:T(8,128)(2,1)}, bf16[2,2,1,64,512]{4,3,1,0,2:T(8,128)(2,1)S(1)}, u32[]{:S(2)}, u32[]{:S(2)}) %collective-permute-start.1) | collective-permute-done | bytes 262176 | tf_op jit(solution)/shard_map/ppermute | solution.py:14
  71.5 32.3 %collective-permute-start.6 = (bf16[2,2,1,64,512]{4,3,1,0,2:T(8,128)(2,1)}, bf16[2,2,1,64,512]{4,3,1,0,2:T(8,128)(2,1)S(1)}, u32[]{:S(2)}, u32[]{:S(2)}) collective-permute-start(bf16[2,2,1,64,512]{4,3,1,0,2:T(8,128)(2,1)} %get-tuple-element.65), channel_id=1, source_target_pairs={{0,2},{2,4},{4,6},{6,8},{8,10},{10,12},{12,14},{14,0},{1,3},{3,5},... | collective-permute-start | bytes 786440 | tf_op jit(solution)/shard_map/ppermute | solution.py:14
  103.9 13.3 %collective-permute-done.3 = bf16[2,2,1,64,512]{4,3,1,0,2:T(8,128)(2,1)S(1)} collective-permute-done((bf16[2,2,1,64,512]{4,3,1,0,2:T(8,128)(2,1)}, bf16[2,2,1,64,512]{4,3,1,0,2:T(8,128)(2,1)S(1)}, u32[]{:S(2)}, u32[]{:S(2)}) %collective-permute-start.3) | collective-permute-done | bytes 262176 | tf_op jit(solution)/shard_map/ppermute | solution.py:14
  117.3 0.8 collective-permute-done.4
  118.7 1.8 copy.13
  120.5 3.3 %conditional.8 = (bf16[2,2,512,512]{3,2,1,0:T(8,128)(2,1)S(1)}) conditional(s32[]{:T(128)} %bitcast.37, (bf16[2,2,512,512]{3,2,1,0:T(8,128)(2,1)S(1)}, bf16[2,2,512,512]{3,2,1,0:T(8,128)(2,1)S(1)}) %tuple.61, (bf16[2,2,512,512]{3,2,1,0:T(8,128)(2,1)S(1)}, bf16[2,2,512,512]{3,2,1,0:T(8,128)(2,1)S(1)}) %tuple.62), branch_computations={%region_4.5_spmd, %region_5.6_spmd} | conditional | flops 2150629376 | bytes 23068680
  120.7 0.7 fusion.72
  121.4 0.7 add_bitcast_fusion.4
  122.1 0.7 fusion.78
  122.8 0.7 subtract_bitcast_fusion.4
  124.0 50.3 %all_to_all.30 = bf16[2,2,8,64,512]{4,3,1,0,2:T(8,128)(2,1)S(1)} all-to-all(bf16[2,2,8,64,512]{4,3,1,0,2:T(8,128)(2,1)S(1)} %copy.16), channel_id=1, replica_groups=mesh['cuts'=2,'mode'=8,'branch'=2] {'mode'}, dimensions={2} | all-to-all | bytes 4194304 | tf_op jit(solution)/shard_map/all_to_all | solution.py:76
  175.2 1.7 slice_bitcast_fusion.9
  176.9 0.3 broadcast_select_fusion
  177.1 1.7 collective-permute-done.7
  178.9 2.0 %broadcast_select_fusion.3 = (bf16[2,2,512,512]{3,2,1,0:T(8,128)(2,1)S(1)}, bf16[2,2,512,512]{3,2,1,0:T(8,128)(2,1)S(1)}, bf16[2,2,512,512]{3,2,1,0:T(8,128)(2,1)S(1)}) fusion(pred[]{:T(512)} %bitcast.36, bf16[2,2,512,512]{3,2,1,0:T(8,128)(2,1)} %collective-permute-done.7, bf16[2,2,512,512]{3,2,1,0:T(8,128)(2,1)S(1)} %bitcast.234, pred[]{:T(512)S(6)} %eq.33), kind=kLoop, calls=%fused_computation.137 | loop fusion | flops 3145728 | bytes 10485762 | tf_op jit(solution)/shard_map/jit(_where)/select_n | solution.py:89
  180.9 0.3 dynamic-slice_select_fusion
  181.2 0.4 fusion.114
  181.6 0.4 fusion.113
  182.1 0.4 fusion.111
  182.5 0.4 fusion.116
  183.0 0.4 fusion.115
  183.4 0.4 fusion.112
  183.9 0.4 fusion.109
  184.3 0.4 fusion.110
  184.7 1.5 pad_maximum_fusion.6
  (40 shorter events, 1.5 us)
Async XLA Ops:
  0.0 5.7 %copy-start.7 = (s32[7]{0:T(128)S(1)}, s32[7]{0:T(128)}, u32[]{:S(2)}) copy-start(s32[7]{0:T(128)} %param.11) | copy-start | bytes 88
  7.0 2.4 %copy-start.3 = (bf16[2,2,512,512]{3,2,1,0:T(8,128)(2,1)S(1)}, bf16[2,2,512,512]{3,2,1,0:T(8,128)(2,1)}, u32[]{:S(2)}) copy-start(bf16[2,2,512,512]{3,2,1,0:T(8,128)(2,1)} %get-tuple-element.46) | copy-start | bytes 6291460 | tf_op jit(solution)/shard_map/conditional
  7.0 2.8 %copy-start.5 = (bf16[2,2,512,512]{3,2,1,0:T(8,128)(2,1)S(1)}, bf16[2,2,512,512]{3,2,1,0:T(8,128)(2,1)}, u32[]{:S(2)}) copy-start(bf16[2,2,512,512]{3,2,1,0:T(8,128)(2,1)} %get-tuple-element.47) | copy-start | bytes 6291460 | tf_op jit(solution)/shard_map/conditional
  16.7 102.0 %all-to-all-start = ((bf16[2,2,8,64,512]{4,3,1,0,2:T(8,128)(2,1)}), bf16[2,2,8,64,512]{4,3,1,0,2:T(8,128)(2,1)}, u32[]{:S(2)}, u32[]{:S(2)}) async-start(bf16[2,2,8,64,512]{4,3,1,0,2:T(8,128)(2,1)} %copy.12), calls=%async_computation | async-start | bytes 4194304 | tf_op jit(solution)/shard_map/all_to_all | solution.py:67
  24.7 2.1 %copy-start = (bf16[2,2,512,512]{3,2,1,0:T(8,128)(2,1)S(1)}, bf16[2,2,512,512]{3,2,1,0:T(8,128)(2,1)}, u32[]{:S(2)}) copy-start(bf16[2,2,512,512]{3,2,1,0:T(8,128)(2,1)} %get-tuple-element.48) | copy-start | bytes 6291460 | tf_op jit(solution)/shard_map/conditional.1
  29.1 1.3 copy-start.6
  34.1 31.8 %collective-permute-start = (bf16[2,2,1,64,512]{4,3,1,0,2:T(8,128)(2,1)}, bf16[2,2,1,64,512]{4,3,1,0,2:T(8,128)(2,1)S(1)}, u32[]{:S(2)}, u32[]{:S(2)}) collective-permute-start(bf16[2,2,1,64,512]{4,3,1,0,2:T(8,128)(2,1)} %get-tuple-element.71), channel_id=1, source_target_pairs={{0,14},{2,0},{4,2},{6,4},{8,6},{10,8},{12,10},{14,12},{1,15},{3,1}... | collective-permute-start | bytes 786440 | tf_op jit(solution)/shard_map/ppermute | solution.py:14
  38.8 32.7 %collective-permute-start.1 = (bf16[2,2,1,64,512]{4,3,1,0,2:T(8,128)(2,1)}, bf16[2,2,1,64,512]{4,3,1,0,2:T(8,128)(2,1)S(1)}, u32[]{:S(2)}, u32[]{:S(2)}) collective-permute-start(bf16[2,2,1,64,512]{4,3,1,0,2:T(8,128)(2,1)} %get-tuple-element.70), channel_id=1, source_target_pairs={{0,12},{2,14},{4,0},{6,2},{8,4},{10,6},{12,8},{14,10},{1,13},{3,15... | collective-permute-start | bytes 786440 | tf_op jit(solution)/shard_map/ppermute | solution.py:14
  39.3 64.5 %collective-permute-start.2 = (bf16[2,2,1,64,512]{4,3,1,0,2:T(8,128)(2,1)}, bf16[2,2,1,64,512]{4,3,1,0,2:T(8,128)(2,1)S(1)}, u32[]{:S(2)}, u32[]{:S(2)}) collective-permute-start(bf16[2,2,1,64,512]{4,3,1,0,2:T(8,128)(2,1)} %get-tuple-element.69), channel_id=1, source_target_pairs={{0,10},{2,12},{4,14},{6,0},{8,2},{10,4},{12,6},{14,8},{1,11},{3,13... | collective-permute-start | bytes 786440 | tf_op jit(solution)/shard_map/ppermute | solution.py:14
  39.3 77.9 %collective-permute-start.3 = (bf16[2,2,1,64,512]{4,3,1,0,2:T(8,128)(2,1)}, bf16[2,2,1,64,512]{4,3,1,0,2:T(8,128)(2,1)S(1)}, u32[]{:S(2)}, u32[]{:S(2)}) collective-permute-start(bf16[2,2,1,64,512]{4,3,1,0,2:T(8,128)(2,1)} %get-tuple-element.68), channel_id=1, source_target_pairs={{0,8},{2,10},{4,12},{6,14},{8,0},{10,2},{12,4},{14,6},{1,9},{3,11}... | collective-permute-start | bytes 786440 | tf_op jit(solution)/shard_map/ppermute | solution.py:14
  42.3 75.8 %collective-permute-start.4 = (bf16[2,2,1,64,512]{4,3,1,0,2:T(8,128)(2,1)}, bf16[2,2,1,64,512]{4,3,1,0,2:T(8,128)(2,1)S(1)}, u32[]{:S(2)}, u32[]{:S(2)}) collective-permute-start(bf16[2,2,1,64,512]{4,3,1,0,2:T(8,128)(2,1)} %get-tuple-element.67), channel_id=1, source_target_pairs={{0,6},{2,8},{4,10},{6,12},{8,14},{10,0},{12,2},{14,4},{1,7},{3,9},... | collective-permute-start | bytes 786440 | tf_op jit(solution)/shard_map/ppermute | solution.py:14
  65.9 52.2 %collective-permute-start.5 = (bf16[2,2,1,64,512]{4,3,1,0,2:T(8,128)(2,1)}, bf16[2,2,1,64,512]{4,3,1,0,2:T(8,128)(2,1)S(1)}, u32[]{:S(2)}, u32[]{:S(2)}) collective-permute-start(bf16[2,2,1,64,512]{4,3,1,0,2:T(8,128)(2,1)} %get-tuple-element.66), channel_id=1, source_target_pairs={{0,4},{2,6},{4,8},{6,10},{8,12},{10,14},{12,0},{14,2},{1,5},{3,7},... | collective-permute-start | bytes 786440 | tf_op jit(solution)/shard_map/ppermute | solution.py:14
  71.5 46.7 %collective-permute-start.6 = (bf16[2,2,1,64,512]{4,3,1,0,2:T(8,128)(2,1)}, bf16[2,2,1,64,512]{4,3,1,0,2:T(8,128)(2,1)S(1)}, u32[]{:S(2)}, u32[]{:S(2)}) collective-permute-start(bf16[2,2,1,64,512]{4,3,1,0,2:T(8,128)(2,1)} %get-tuple-element.65), channel_id=1, source_target_pairs={{0,2},{2,4},{4,6},{6,8},{8,10},{10,12},{12,14},{14,0},{1,3},{3,5},... | collective-permute-start | bytes 786440 | tf_op jit(solution)/shard_map/ppermute | solution.py:14
  174.3 0.9 copy-start.8
  174.5 4.4 %collective-permute-start.7 = (bf16[2,2,512,512]{3,2,1,0:T(8,128)(2,1)S(1)}, bf16[2,2,512,512]{3,2,1,0:T(8,128)(2,1)}, u32[]{:S(2)}, u32[]{:S(2)}) collective-permute-start(bf16[2,2,512,512]{3,2,1,0:T(8,128)(2,1)S(1)} %bitcast.233), channel_id=1, source_target_pairs={{0,1},{1,0},{2,3},{3,2},{4,5},{5,4},{6,7},{7,6},{8,9},{9,8},{10,11... | collective-permute-start | bytes 6291464 | tf_op jit(solution)/shard_map/ppermute | solution.py:22
